TPU v7x, 32 devices: a whole 2x2x4 slice. The times are simulated.
32 devices in a mesh: ctx: 8 (over z, x), tp: 4 (over y, core).
Axes of the slice: x: 2, y: 2, z: 4, core: 2. Of those that a mesh axis runs over, the one named last changes fastest.
Arguments:
- residual: bfloat16 [1024, 4096], P('ctx', 'tp')
- mixer_input: bfloat16 [1024, 4096], P('ctx', 'tp')
- gate_input: bfloat16 [1024, 4096], P('ctx', 'tp'), may hold values from -6 to 6
- state_proj: bfloat16 [1024, 32], P('ctx'), may hold values from -6 to 6
- step_raw: float32 [1024, 64], P('ctx', 'tp'), may hold values from -5 to 5
- conv_weight: float32 [4, 4096], P(None, 'tp'), may hold values from -3 to 3
- conv_state_weight: float32 [4, 32], replicated, may hold values from -3 to 3
- step_bias: float32 [64], P('tp'), may hold values from -3.5 to 0.5
- decay_log: float32 [64], P('tp')
- skip_gain: float32 [64], P('tp'), may hold values from 0.5 to 1.5
- mixer_gain: float32 [4096], P('tp'), may hold values from 0.5 to 1.5
- out_weight: bfloat16 [4096, 4096], P('tp', 'ctx'), may hold values from -0.09375 to 0.09375
- feed_gain: float32 [4096], P('tp'), may hold values from 0.5 to 1.5
- expert_gate: bfloat16 [8, 4096, 7168], P('ctx', 'tp'), may hold values from -0.09375 to 0.09375
- expert_up: bfloat16 [8, 4096, 7168], P('ctx', 'tp'), may hold values from -0.09375 to 0.09375
- expert_down: bfloat16 [8, 7168, 4096], P('ctx', None, 'tp'), may hold values from -0.0625 to 0.0625
- expert_ids: int32 [1024, 2], P('ctx'), may hold values from 0 to 7, all different within a row; in each aligned block of 128 rows (0 to 127, 128 to 255, ...) at most 36 rows name the same one
- expert_weights: float32 [1024, 2], P('ctx'), may hold values from 0.1 to 0.9
Outputs:
- block_out: bfloat16 [1024, 4096], P('ctx', 'tp')
Inputs may be any that keep to these rules, and one draw needn't show every extreme that they name: `expert_ids`: in each aligned block of 128 rows no expert is named more than 36 times, and some block reaches 36; the two experts of a row differ.
All inputs are finite; a program needn't handle non-finite values.
Results may differ from a plain program's by a relative error of at most 0.014.
Values may be sent and summed in bfloat16 or wider, within the bound.
A program may use at most 128 MiB of HBM per device.

v0:
```python
import jax
import jax.numpy as jnp
from jax import lax
from jax.sharding import PartitionSpec as P

EXPERTS = 8
CAP = 36


EPSILON = 1e-05


def passed_along(value, axis, steps):
    count = lax.axis_size(axis)
    first, last = (max(0, -steps), min(count, count - steps))
    return lax.ppermute(value, axis, [(source, source + steps) for source in range(first, last)])


def entering(x, axis, combine, identity):
    peers, position = (lax.axis_size(axis), lax.axis_index(axis))
    everything = jax.tree.map(
        lambda part, kind: lax.all_gather(part.astype(kind), axis), x, (jnp.bfloat16, jnp.bfloat16)
    )
    start = jax.tree.map(
        lambda part, zero: jnp.broadcast_to(jnp.asarray(zero, part.dtype), part.shape), x, identity
    )

    def step(k, before):
        reached = k < position
        new = combine(
            before, jax.tree.map(lambda part, own: part[k].astype(own.dtype), everything, x)
        )
        return jax.tree.map(lambda a, b: jnp.where(reached, a, b), new, before)

    return lax.fori_loop(0, peers, step, start)


def causal_filter(previous, current, kernel):
    joined = jnp.concatenate([previous, current], axis=0)
    length = current.shape[0]
    total = jnp.zeros(current.shape, jnp.float32)
    for offset in range(kernel.shape[0]):
        total = total + kernel[offset][None, :] * joined[offset : offset + length]
    return jax.nn.silu(total)


def local_terms(values, writer, reader, step_size, log_decay):
    length = values.shape[0]
    cumulative = jnp.cumsum(log_decay, axis=0)
    scores = jnp.dot(reader, writer.T, precision=lax.Precision.HIGHEST)
    order = jnp.arange(length)
    causal = (order[:, None] >= order[None, :])[:, :, None]
    spans = cumulative[:, None, :] - cumulative[None, :, :]
    factor = jnp.where(causal, jnp.exp(jnp.where(causal, spans, 0.0)), 0.0)
    factor = factor * step_size[None, :, :] * scores[:, :, None]
    inside = jnp.einsum("tsh,shp->thp", factor, values, precision=lax.Precision.HIGHEST)
    tail = cumulative[length - 1]
    ending = jnp.exp(tail[None, :] - cumulative) * step_size
    fresh = jnp.einsum("th,thp,tn->hpn", ending, values, writer, precision=lax.Precision.HIGHEST)
    return (inside, cumulative, fresh, tail)


def body(
    residual,
    mixer_input,
    gate_input,
    state_proj,
    step_raw,
    conv_weight,
    conv_state_weight,
    step_bias,
    decay_log,
    skip_gain,
    mixer_gain,
    out_weight,
    feed_gain,
    expert_gate,
    expert_up,
    expert_down,
    expert_ids,
    expert_weights,
):
    tensor_count = lax.axis_size("tp")
    context_count = lax.axis_size("ctx")
    tokens = mixer_input.shape[0]
    channels = mixer_input.shape[1]
    states = state_proj.shape[1] // 2
    heads_local = step_raw.shape[1]
    head_size = channels // heads_local
    taps = conv_weight.shape[0]
    joined = jnp.concatenate([mixer_input, state_proj], axis=1)
    previous = passed_along(joined[tokens - (taps - 1) :], "ctx", 1)
    kernel = jnp.concatenate([conv_weight, conv_state_weight], axis=1)
    filtered = causal_filter(previous.astype(jnp.float32), joined.astype(jnp.float32), kernel)
    values = filtered[:, :channels].reshape(tokens, heads_local, head_size)
    writer = filtered[:, channels : channels + states]
    reader = filtered[:, channels + states :]
    step_size = jax.nn.softplus(step_raw + step_bias[None, :])
    log_decay = -step_size * jnp.exp(decay_log)[None, :]
    inside, cumulative, fresh, tail = local_terms(values, writer, reader, step_size, log_decay)

    def combine(earlier, later):
        return (earlier[0] * later[0], later[0][:, None, None] * earlier[1] + later[1])

    prefix = entering(
        (jnp.exp(tail), fresh), "ctx", combine, (jnp.ones_like(tail), jnp.zeros_like(fresh))
    )
    incoming = prefix[1]
    carried = (
        jnp.einsum("tn,hpn->thp", reader, incoming, precision=lax.Precision.HIGHEST)
        * jnp.exp(cumulative)[:, :, None]
    )
    mixed = inside + carried + skip_gain[None, :, None] * values
    gated = mixed.reshape(tokens, channels) * jax.nn.silu(gate_input.astype(jnp.float32))
    square_sum = lax.psum(jnp.sum(gated * gated, axis=1), "tp")
    scale = lax.rsqrt(square_sum / (channels * tensor_count) + EPSILON)
    normed = (gated * scale[:, None] * mixer_gain[None, :]).astype(jnp.bfloat16)
    partial_value = jnp.dot(
        normed,
        lax.all_gather(out_weight, "ctx", axis=1, tiled=True),
        preferred_element_type=jnp.float32,
    )
    mixer_out = lax.psum_scatter(
        partial_value.astype(jnp.bfloat16), "tp", scatter_dimension=1, tiled=True
    ).astype(jnp.float32)
    hidden_state = (residual.astype(jnp.float32) + mixer_out).astype(jnp.bfloat16)
    state_float = lax.optimization_barrier(hidden_state).astype(jnp.float32)
    width_total = hidden_state.shape[1] * tensor_count
    feed_sum = lax.psum(jnp.sum(state_float * state_float, axis=1), "tp")
    feed_scale = lax.rsqrt(feed_sum / width_total + EPSILON)
    expert_input = (state_float * feed_scale[:, None] * feed_gain[None, :]).astype(jnp.bfloat16)
    group = context_count // EXPERTS
    width_local = expert_input.shape[1]
    flat_experts = expert_ids.reshape(-1)
    matches = (flat_experts[:, None] == jnp.arange(EXPERTS)[None, :]).astype(jnp.int32)
    slots = jnp.sum((jnp.cumsum(matches, axis=0) - matches) * matches, axis=1)
    targets = (flat_experts * CAP + slots).reshape(tokens, -1)
    picker = jnp.any(targets[None, :, :] == jnp.arange(EXPERTS * CAP)[:, None, None], axis=2)
    buffer = jnp.dot(
        picker.astype(jnp.bfloat16), expert_input, preferred_element_type=jnp.float32
    ).astype(jnp.bfloat16)
    outgoing = jnp.broadcast_to(
        buffer.reshape(EXPERTS, 1, CAP, width_local), (EXPERTS, group, CAP, width_local)
    )
    outgoing = outgoing.reshape(EXPERTS * group, CAP, width_local)
    gate_local = expert_gate[0]
    up_local = expert_up[0]
    down_local = expert_down[0]
    arrived = lax.all_to_all(outgoing, "ctx", split_axis=0, concat_axis=0, tiled=True)
    sources, items, depth = arrived.shape
    flattened = arrived.reshape(sources * items, depth)
    gate_part = jnp.dot(flattened, gate_local, preferred_element_type=jnp.float32)
    up_part = jnp.dot(flattened, up_local, preferred_element_type=jnp.float32)
    gate_share = lax.psum_scatter(
        gate_part.astype(jnp.bfloat16), "tp", scatter_dimension=1, tiled=True
    ).astype(jnp.float32)
    up_share = lax.psum_scatter(
        up_part.astype(jnp.bfloat16), "tp", scatter_dimension=1, tiled=True
    ).astype(jnp.float32)
    share = (jax.nn.silu(gate_share) * up_share).astype(jnp.bfloat16)
    activated = lax.all_gather(share, "tp", axis=1, tiled=True)
    answer = jnp.dot(activated, down_local, preferred_element_type=jnp.float32).astype(jnp.bfloat16)
    answers = lax.all_to_all(
        answer.reshape(sources, items, depth), "ctx", split_axis=0, concat_axis=0, tiled=True
    )
    summed = jnp.sum(answers.reshape(EXPERTS, group, CAP, width_local), axis=1, dtype=jnp.float32)
    summed = summed.reshape(EXPERTS * CAP, width_local)
    chosen = jnp.take(summed, targets, axis=0)
    routed = jnp.sum(expert_weights[:, :, None] * chosen, axis=1)
    return (state_float + routed).astype(jnp.bfloat16)


def solution(mesh):
    placed = (
        P("ctx", "tp"),
        P("ctx", "tp"),
        P("ctx", "tp"),
        P("ctx", None),
        P("ctx", "tp"),
        P(None, "tp"),
        P(),
        P("tp"),
        P("tp"),
        P("tp"),
        P("tp"),
        P("tp", "ctx"),
        P("tp"),
        P("ctx", "tp", None),
        P("ctx", "tp", None),
        P("ctx", None, "tp"),
        P("ctx", None),
        P("ctx", None),
    )
    return jax.shard_map(
        body, mesh=mesh, in_specs=placed, out_specs=P("ctx", "tp"), check_vma=False
    )
```

profile of v0, /device:TPU:0, one launch (start us, length us, event | category | flops | bytes accessed | tf_op | source)
XLA Modules:
  0.0 383.7 jit_solution(1785085209959338973)
XLA Ops:
  6.5 0.7 all-gather.5.cloned.1.call-update
  7.3 1.1 copy.70
  8.4 0.8 fusion.53
  9.3 4.9 %collective-permute-start = (bf16[3,1056]{0,1:T(8,128)(2,1)S(1)}, bf16[3,1056]{0,1:T(8,128)(2,1)S(1)}, u32[]{:S(2)}, u32[]{:S(2)}) collective-permute-start(bf16[3,1056]{0,1:T(8,128)(2,1)S(1)} %fusion.53), channel_id=1, source_target_pairs={{0,4},{4,8},{8,12},{12,16},{16,20},{20,24},{24,28},{1,5},{5,9},{9,... | collective-permute-start | bytes 19016 | tf_op jit(solution)/shard_map/ppermute | solution.py:16
  14.2 0.7 exp.38
  14.8 0.8 negate_multiply_fusion
  15.7 0.2 reduce_window_sum.26
  16.0 0.7 constant_dynamic-update-slice_fusion.1
  16.7 0.7 constant_dynamic-update-slice_fusion
  17.5 0.8 fusion.52
  18.3 19.2 %all-gather.1 = bf16[8,1,16]{2,1,0:T(2,128)(2,1)S(1)} all-gather(bf16[1,1,16]{2,1,0:T(2,128)(2,1)S(1)} %get-tuple-element.137), channel_id=1, replica_groups=mesh['ctx'=8,'tp'=4] {'ctx'}, dimensions={0}, use_global_device_ids=true | all-gather | bytes 288 | tf_op jit(solution)/shard_map/all_gather | solution.py:22
  37.6 1.5 divide_multiply_fusion
  39.2 0.9 convolution_convert_fusion.2
  40.1 33.4 %all-gather = bf16[128,64,16]{1,2,0:T(8,128)(2,1)S(1)} all-gather(bf16[16,64,16]{1,2,0:T(8,128)(2,1)S(1)} %convolution_convert_fusion.2), channel_id=2, replica_groups=mesh['ctx'=8,'tp'=4] {'ctx'}, dimensions={0}, use_global_device_ids=true | all-gather | bytes 294912 | tf_op jit(solution)/shard_map/all_gather | solution.py:22
  73.5 0.3 fusion.67
  73.8 1.1 while.14
  74.9 1.0 convolution_multiply_fusion
  75.9 2.3 fusion.22
  78.2 0.2 copy.76
  78.4 0.2 multiply_reduce_fusion.1
  78.6 6.1 %psum.14 = f32[128]{0:T(128)S(1)} all-reduce(f32[128]{0:T(128)S(1)} %multiply_reduce_fusion.1), channel_id=1, replica_groups=mesh['ctx'=8,'tp'=4] {'tp'}, use_global_device_ids=true, to_apply=%region_4.5 | all-reduce | flops 128 | bytes 1024 | tf_op jit(solution)/shard_map/psum | solution.py:115
  84.7 56.5 %all-gather.5.cloned.1.call-done = bf16[1024,4096]{1,0:T(8,128)(2,1)} async-done(((bf16[1024,512]{1,0:T(8,128)(2,1)}), bf16[1024,4096]{1,0:T(8,128)(2,1)}) %all-gather.5.cloned.1.call-update) | async-done | bytes 8388624 | tf_op jit(solution)/shard_map/all_gather | solution.py:120
  141.3 5.9 %convolution_convert_fusion = bf16[128,4096]{1,0:T(8,128)(2,1)} fusion(bf16[1024,4096]{1,0:T(8,128)(2,1)} %all-gather.5.cloned.1.call-done, f32[1024]{0:T(1024)S(1)} %copy-done.5, f32[128]{0:T(128)S(1)} %add_rsqrt_fusion.1, f32[128,1024]{1,0:T(8,128)S(1)} %copy.76, bf16[128,1024]{1,0:T(8,128)(2,1)S(1)} %copy-done.1), kind=kOutput, calls=%fused_computation.12 | convolution fusion | flops 1075445760 | bytes 10228224 | tf_op jit(solution)/shard_map/dot_general | solution.py:118
  147.5 0.1 eq.38
  147.6 0.6 reduce-window.6
  148.2 0.2 slice_reduce_fusion
  148.6 0.1 reduce_sum.44
  148.8 21.8 %reduce-scatter.4.cloned.1.call-done = bf16[128,1024]{1,0:T(8,128)(2,1)} async-done(((bf16[128,4096]{1,0:T(8,128)(2,1)}), bf16[128,1024]{1,0:T(8,128)(2,1)}) %reduce-scatter.4.cloned.1.call-update) | async-done | bytes 262160 | tf_op jit(solution)/shard_map/reduce_scatter | solution.py:123
  170.6 1.0 add_convert_fusion
  171.8 5.8 %psum.15 = f32[128]{0:T(128)S(1)} all-reduce(f32[128]{0:T(128)S(1)} %fusion.41), channel_id=1, replica_groups=mesh['ctx'=8,'tp'=4] {'tp'}, use_global_device_ids=true, to_apply=%region_11.12 | all-reduce | flops 128 | bytes 1024 | tf_op jit(solution)/shard_map/psum | solution.py:129
  177.6 0.4 convolution_convert_fusion.1
  178.1 23.0 %all_to_all.10 = bf16[8,36,1024]{2,1,0:T(8,128)(2,1)S(1)} all-to-all(bf16[8,36,1024]{2,1,0:T(8,128)(2,1)S(1)} %reshape_reshape.3), channel_id=1, replica_groups=mesh['ctx'=8,'tp'=4] {'ctx'}, dimensions={0} | all-to-all | bytes 1179648 | tf_op jit(solution)/shard_map/all_to_all | solution.py:149
  201.2 11.1 %fusion.7 = bf16[288,7168]{1,0:T(8,128)(2,1)} fusion(bf16[288,1024]{1,0:T(8,128)(2,1)S(1)} %reshape.95, bf16[1,1024,7168]{2,1,0:T(8,128)(2,1)} %param.33), kind=kOutput, calls=%fused_computation.10 | convolution fusion | flops 4229922816 | bytes 19398656 | tf_op jit(solution)/shard_map/dot_general | solution.py:152
  212.3 0.2 reduce-scatter.8.cloned.1.call-start
  212.6 12.3 %fusion.10 = bf16[288,7168]{1,0:T(8,128)(2,1)} fusion(bf16[288,1024]{1,0:T(8,128)(2,1)S(1)} %reshape.95, bf16[1,1024,7168]{2,1,0:T(8,128)(2,1)} %param.34), kind=kOutput, calls=%fused_computation.11 | convolution fusion | flops 4229922816 | bytes 19398656 | tf_op jit(solution)/shard_map/dot_general | solution.py:153
  225.0 29.2 %reduce-scatter.6.cloned.1.call-done = bf16[288,1792]{1,0:T(8,128)(2,1)} async-done(((bf16[288,7168]{1,0:T(8,128)(2,1)}), bf16[288,1792]{1,0:T(8,128)(2,1)}) %reduce-scatter.6.cloned.1.call-update) | async-done | bytes 1032208 | tf_op jit(solution)/shard_map/reduce_scatter | solution.py:154
  254.2 46.4 %reduce-scatter.8.cloned.1.call-done = bf16[288,1792]{1,0:T(8,128)(2,1)} async-done(((bf16[288,7168]{1,0:T(8,128)(2,1)}), bf16[288,1792]{1,0:T(8,128)(2,1)}) %reduce-scatter.8.cloned.1.call-update) | async-done | bytes 1032208 | tf_op jit(solution)/shard_map/reduce_scatter | solution.py:157
  300.6 3.1 fusion.17
  303.8 34.2 %all-gather.7.cloned.1.call-done = bf16[288,7168]{1,0:T(8,128)(2,1)} async-done(((bf16[288,1792]{1,0:T(8,128)(2,1)}), bf16[288,7168]{1,0:T(8,128)(2,1)}) %all-gather.7.cloned.1.call-update) | async-done | bytes 4128784 | tf_op jit(solution)/shard_map/all_gather | solution.py:161
  338.0 10.8 %fusion.18 = bf16[288,1024]{1,0:T(8,128)(2,1)S(1)} fusion(bf16[288,7168]{1,0:T(8,128)(2,1)} %all-gather.7.cloned.1.call-done, bf16[1,7168,1024]{2,1,0:T(8,128)(2,1)} %param.35), kind=kOutput, calls=%fused_computation.20 | convolution fusion | flops 4228153344 | bytes 19398656 | tf_op jit(solution)/shard_map/dot_general | solution.py:162
  348.9 0.9 reshape.96
  349.8 5.5 %all-to-all-start.1 = ((bf16[8,36,1024]{2,1,0:T(8,128)(2,1)}), bf16[8,36,1024]{2,1,0:T(8,128)(2,1)S(1)}, u32[]{:S(2)}, u32[]{:S(2)}) async-start(bf16[8,36,1024]{2,1,0:T(8,128)(2,1)} %reshape.96), calls=%async_computation.4 | async-start | bytes 1310720 | tf_op jit(solution)/shard_map/all_to_all | solution.py:163
  355.6 0.1 copy.81
  355.9 17.2 %all-to-all-done.1 = bf16[8,36,1024]{2,1,0:T(8,128)(2,1)S(1)} async-done(((bf16[8,36,1024]{2,1,0:T(8,128)(2,1)}), bf16[8,36,1024]{2,1,0:T(8,128)(2,1)S(1)}, u32[]{:S(2)}, u32[]{:S(2)}) %all-to-all-start.1) | async-done | bytes 589856 | tf_op jit(solution)/shard_map/all_to_all | solution.py:163
  373.1 1.1 gather_fusion
  374.2 0.6 reshape.104
  374.8 1.5 multiply_reduce_fusion
  376.4 0.8 fusion.44
  (72 shorter events, 2.9 us)
Async XLA Ops:
  6.5 134.7 %all-gather.5.cloned.1.call-start = ((), (), s32[]{:S(2)}) async-start(), calls=%async_computation.5 | async-start | bytes 9437184 | tf_op jit(solution)/shard_map/all_gather | solution.py:120
  7.3 163.4 %reduce-scatter.4.cloned.1.call-start = ((), (), s32[]{:S(2)}) async-start(), calls=%async_computation.6 | async-start | bytes 1310720 | tf_op jit(solution)/shard_map/reduce_scatter | solution.py:123
  9.3 28.3 %collective-permute-start = (bf16[3,1056]{0,1:T(8,128)(2,1)S(1)}, bf16[3,1056]{0,1:T(8,128)(2,1)S(1)}, u32[]{:S(2)}, u32[]{:S(2)}) collective-permute-start(bf16[3,1056]{0,1:T(8,128)(2,1)S(1)} %fusion.53), channel_id=1, source_target_pairs={{0,4},{4,8},{8,12},{12,16},{16,20},{20,24},{24,28},{1,5},{5,9},{9,... | collective-permute-start | bytes 19016 | tf_op jit(solution)/shard_map/ppermute | solution.py:16
  17.5 58.4 %copy-start.6 = (f32[16]{0:T(128)S(1)}, f32[16]{0:T(128)}, u32[]{:S(2)}) copy-start(f32[16]{0:T(128)} %param.29) | copy-start | bytes 196
  39.1 39.3 %copy-start.1 = (bf16[128,1024]{1,0:T(8,128)(2,1)S(1)}, bf16[128,1024]{1,0:T(8,128)(2,1)}, u32[]{:S(2)}) copy-start(bf16[128,1024]{1,0:T(8,128)(2,1)} %param.22) | copy-start | bytes 786436
  39.2 102.1 %copy-start.5 = (f32[1024]{0:T(1024)S(1)}, f32[1024]{0:T(1024)}, u32[]{:S(2)}) copy-start(f32[1024]{0:T(1024)} %param.30) | copy-start | bytes 12292
  84.7 62.5 %copy-start.3 = (s32[128,2]{0,1:T(2,128)S(1)}, s32[128,2]{0,1:T(2,128)}, u32[]{:S(2)}) copy-start(s32[128,2]{0,1:T(2,128)} %param.36) | copy-start | bytes 3076
  84.7 85.9 %copy-start = (bf16[128,1024]{1,0:T(8,128)(2,1)S(1)}, bf16[128,1024]{1,0:T(8,128)(2,1)}, u32[]{:S(2)}) copy-start(bf16[128,1024]{1,0:T(8,128)(2,1)} %param.20) | copy-start | bytes 786436
  84.7 92.8 %copy-start.2 = (f32[1024]{0:T(1024)S(1)}, f32[1024]{0:T(1024)}, u32[]{:S(2)}) copy-start(f32[1024]{0:T(1024)} %param.32) | copy-start | bytes 12292
  147.1 107.0 %reduce-scatter.6.cloned.1.call-start = ((), (), s32[]{:S(2)}) async-start(), calls=%async_computation.7 | async-start | bytes 5160960 | tf_op jit(solution)/shard_map/reduce_scatter | solution.py:154
  212.3 88.3 %reduce-scatter.8.cloned.1.call-start = ((), (), s32[]{:S(2)}) async-start(), calls=%async_computation.8 | async-start | bytes 5160960 | tf_op jit(solution)/shard_map/reduce_scatter | solution.py:157
  224.9 113.1 %all-gather.7.cloned.1.call-start = ((), (), s32[]{:S(2)}) async-start(), calls=%async_computation.9 | async-start | bytes 5160960 | tf_op jit(solution)/shard_map/all_gather | solution.py:161
  303.8 51.9 %copy-start.4 = (f32[128,2]{0,1:T(2,128)S(1)}, f32[128,2]{0,1:T(2,128)}, u32[]{:S(2)}) copy-start(f32[128,2]{0,1:T(2,128)} %param.37) | copy-start | bytes 3076
  349.8 23.2 %all-to-all-start.1 = ((bf16[8,36,1024]{2,1,0:T(8,128)(2,1)}), bf16[8,36,1024]{2,1,0:T(8,128)(2,1)S(1)}, u32[]{:S(2)}, u32[]{:S(2)}) async-start(bf16[8,36,1024]{2,1,0:T(8,128)(2,1)} %reshape.96), calls=%async_computation.4 | async-start | bytes 1310720 | tf_op jit(solution)/shard_map/all_to_all | solution.py:163
Sparse Core Ops, SparseCore 0:
  9.4 131.8 all-gather.4
  147.3 23.3 reduce-scatter.3
  212.4 41.6 reduce-scatter.5
  256.6 43.9 reduce-scatter.7
  303.9 34.0 all-gather.6
where the time goes:
time: 384 us
  waiting for transfers between devices  206 us (54%)
  blocking collectives  87.3 us (23%)
  matrix products  45.1 us (12%)
  between operations  13.5 us (4%)
  other arithmetic  12.6 us (3%)
  starting transfers between devices  10.7 us (3%)
  local copies, waits for them, and re-layouts  8.04 us (2%)
    all_gather x1, waiting for transfers between devices, body(): lax.all_gather(out_weight, 'ctx', axis=1, tiled=True)  56.5 us
    all_gather x2, blocking collectives, entering(): lax.all_gather(part.astype(kind), axis)  52.6 us
    reduce_scatter x1, waiting for transfers between devices, body(): lax.psum_scatter(up_part.astype(jnp.bfloat16), 'tp', scatter_dimension=1,...  46.4 us
    all_gather x1, waiting for transfers between devices, body(): activated = lax.all_gather(share, 'tp', axis=1, tiled=True)  34.2 us
    reduce_scatter x1, waiting for transfers between devices, body(): lax.psum_scatter(gate_part.astype(jnp.bfloat16), 'tp', scatter_dimension=...  29.2 us
    all_to_all x1, blocking collectives, body(): lax.all_to_all(outgoing, 'ctx', split_axis=0, concat_axis=0, tiled=True)  23 us
    reduce_scatter x1, waiting for transfers between devices, body(): lax.psum_scatter(partial_value.astype(jnp.bfloat16), 'tp', scatter_dimens...  21.8 us
    all_to_all x1, waiting for transfers between devices, body(): lax.all_to_all(answer.reshape(sources, items, depth), 'ctx', split_axis=0...  17.2 us
  transfers between devices with their start and end apart: 7, of which 6 were waited for; matrix products, arithmetic and copies ran while one was open for 7% of the time, Pallas kernels for 0%

commit v1 on v0

--- a/solution.py
+++ b/solution.py
@@ -16,23 +16,20 @@
     return lax.ppermute(value, axis, [(source, source + steps) for source in range(first, last)])
 
 
-def entering(x, axis, combine, identity):
+def swapped(value, distance):
+    return lax.ppermute(value, "tp", [(p, p ^ distance) for p in range(lax.axis_size("tp"))])
+
+
+def entering(decay, fresh, axis):
     peers, position = (lax.axis_size(axis), lax.axis_index(axis))
-    everything = jax.tree.map(
-        lambda part, kind: lax.all_gather(part.astype(kind), axis), x, (jnp.bfloat16, jnp.bfloat16)
-    )
-    start = jax.tree.map(
-        lambda part, zero: jnp.broadcast_to(jnp.asarray(zero, part.dtype), part.shape), x, identity
-    )
+    packed = jnp.concatenate([fresh, decay[None, :]], axis=0).astype(jnp.bfloat16)
+    everything = lax.all_gather(packed, axis).astype(jnp.float32)
 
     def step(k, before):
-        reached = k < position
-        new = combine(
-            before, jax.tree.map(lambda part, own: part[k].astype(own.dtype), everything, x)
-        )
-        return jax.tree.map(lambda a, b: jnp.where(reached, a, b), new, before)
-
-    return lax.fori_loop(0, peers, step, start)
+        part = everything[k]
+        return jnp.where(k < position, part[-1:] * before + part[:-1], before)
+
+    return lax.fori_loop(0, peers, step, jnp.zeros_like(fresh))
 
 
 def causal_filter(previous, current, kernel):
@@ -56,7 +53,8 @@
     inside = jnp.einsum("tsh,shp->thp", factor, values, precision=lax.Precision.HIGHEST)
     tail = cumulative[length - 1]
     ending = jnp.exp(tail[None, :] - cumulative) * step_size
-    fresh = jnp.einsum("th,thp,tn->hpn", ending, values, writer, precision=lax.Precision.HIGHEST)
+    weighted = (ending[:, :, None] * values).reshape(length, -1)
+    fresh = jnp.dot(writer.T, weighted, precision=lax.Precision.HIGHEST)
     return (inside, cumulative, fresh, tail)
 
 
@@ -99,30 +97,54 @@
     log_decay = -step_size * jnp.exp(decay_log)[None, :]
     inside, cumulative, fresh, tail = local_terms(values, writer, reader, step_size, log_decay)
 
-    def combine(earlier, later):
-        return (earlier[0] * later[0], later[0][:, None, None] * earlier[1] + later[1])
-
-    prefix = entering(
-        (jnp.exp(tail), fresh), "ctx", combine, (jnp.ones_like(tail), jnp.zeros_like(fresh))
-    )
-    incoming = prefix[1]
+    incoming = entering(jnp.repeat(jnp.exp(tail), head_size), fresh, "ctx")
     carried = (
-        jnp.einsum("tn,hpn->thp", reader, incoming, precision=lax.Precision.HIGHEST)
+        jnp.dot(reader, incoming, precision=lax.Precision.HIGHEST).reshape(values.shape)
         * jnp.exp(cumulative)[:, :, None]
     )
     mixed = inside + carried + skip_gain[None, :, None] * values
     gated = mixed.reshape(tokens, channels) * jax.nn.silu(gate_input.astype(jnp.float32))
+    tp_index = lax.axis_index("tp")
+    core, chip = (tp_index % 2, tp_index // 2)
+    everyone = lax.all_gather(
+        (gated * mixer_gain[None, :]).astype(jnp.bfloat16), "ctx", axis=0, tiled=True
+    )
     square_sum = lax.psum(jnp.sum(gated * gated, axis=1), "tp")
     scale = lax.rsqrt(square_sum / (channels * tensor_count) + EPSILON)
-    normed = (gated * scale[:, None] * mixer_gain[None, :]).astype(jnp.bfloat16)
-    partial_value = jnp.dot(
-        normed,
-        lax.all_gather(out_weight, "ctx", axis=1, tiled=True),
-        preferred_element_type=jnp.float32,
-    )
-    mixer_out = lax.psum_scatter(
-        partial_value.astype(jnp.bfloat16), "tp", scatter_dimension=1, tiled=True
-    ).astype(jnp.float32)
+    span = everyone.shape[0] // tensor_count
+
+    def projected(quarter):
+        rows = lax.dynamic_slice_in_dim(everyone, quarter * span, span, 0)
+        return jnp.dot(rows, out_weight, preferred_element_type=jnp.float32)
+
+    own, beside = (chip * 2 + core, chip * 2 + 1 - core)
+    across, diagonal = ((1 - chip) * 2 + core, (1 - chip) * 2 + 1 - core)
+    far = swapped(projected(diagonal).astype(jnp.bfloat16), 1)
+    far = swapped((projected(across) + far.astype(jnp.float32)).astype(jnp.bfloat16), 2)
+    near = swapped(projected(beside).astype(jnp.bfloat16), 1)
+    reduced = projected(own) + near.astype(jnp.float32) + far.astype(jnp.float32)
+    blocks = context_count // tensor_count
+    reduced = reduced.astype(jnp.bfloat16).reshape(blocks, tokens, -1)
+    ctx_index = lax.axis_index("ctx")
+    pieces = []
+    for j in range(blocks):
+        moves = [
+            (c * tensor_count + p, (p * blocks + (c + j) % blocks) * tensor_count + c // blocks)
+            for c in range(context_count)
+            for p in range(tensor_count)
+        ]
+        block = lax.dynamic_index_in_dim(reduced, (ctx_index + j) % blocks, 0, keepdims=False)
+        pieces.append(lax.ppermute(block, ("ctx", "tp"), moves))
+    stacked = jnp.stack(pieces)
+    order = (ctx_index - jnp.arange(blocks)) % blocks
+    if blocks == 2:
+        first = ctx_index % 2 == 0
+        mixer_out = jnp.concatenate(
+            [jnp.where(first, pieces[0], pieces[1]), jnp.where(first, pieces[1], pieces[0])], axis=1
+        )
+    else:
+        mixer_out = jnp.take(stacked, order, axis=0).transpose(1, 0, 2).reshape(tokens, -1)
+    mixer_out = mixer_out.astype(jnp.float32) * scale[:, None]
     hidden_state = (residual.astype(jnp.float32) + mixer_out).astype(jnp.bfloat16)
     state_float = lax.optimization_barrier(hidden_state).astype(jnp.float32)
     width_total = hidden_state.shape[1] * tensor_count
@@ -149,17 +171,40 @@
     arrived = lax.all_to_all(outgoing, "ctx", split_axis=0, concat_axis=0, tiled=True)
     sources, items, depth = arrived.shape
     flattened = arrived.reshape(sources * items, depth)
-    gate_part = jnp.dot(flattened, gate_local, preferred_element_type=jnp.float32)
-    up_part = jnp.dot(flattened, up_local, preferred_element_type=jnp.float32)
-    gate_share = lax.psum_scatter(
-        gate_part.astype(jnp.bfloat16), "tp", scatter_dimension=1, tiled=True
-    ).astype(jnp.float32)
-    up_share = lax.psum_scatter(
-        up_part.astype(jnp.bfloat16), "tp", scatter_dimension=1, tiled=True
-    ).astype(jnp.float32)
+    hidden = gate_local.shape[1] // tensor_count
+
+    def product(weight, quarter):
+        columns = lax.dynamic_slice_in_dim(weight, quarter * hidden, hidden, 1)
+        return jnp.dot(flattened, columns, preferred_element_type=jnp.float32)
+
+    weights = (gate_local, up_local)
+    fars = []
+    for weight in weights:
+        far = swapped(product(weight, diagonal).astype(jnp.bfloat16), 1)
+        far = (product(weight, across) + far.astype(jnp.float32)).astype(jnp.bfloat16)
+        fars.append(swapped(far, 2))
+    nears = [swapped(product(weight, beside).astype(jnp.bfloat16), 1) for weight in weights]
+    gate_share, up_share = (
+        product(weight, own).astype(jnp.bfloat16).astype(jnp.float32)
+        + near.astype(jnp.float32)
+        + far.astype(jnp.float32)
+        for weight, near, far in zip(weights, nears, fars)
+    )
     share = (jax.nn.silu(gate_share) * up_share).astype(jnp.bfloat16)
-    activated = lax.all_gather(share, "tp", axis=1, tiled=True)
-    answer = jnp.dot(activated, down_local, preferred_element_type=jnp.float32).astype(jnp.bfloat16)
+    share_across = swapped(share, 2)
+    share_beside = swapped(share, 1)
+    share_diagonal = swapped(share_across, 1)
+
+    def lowered(part, quarter):
+        rows = lax.dynamic_slice_in_dim(down_local, quarter * hidden, hidden, 0)
+        return jnp.dot(part, rows, preferred_element_type=jnp.float32)
+
+    answer = (
+        lowered(share, own)
+        + lowered(share_beside, beside)
+        + lowered(share_across, across)
+        + lowered(share_diagonal, diagonal)
+    ).astype(jnp.bfloat16)
     answers = lax.all_to_all(
         answer.reshape(sources, items, depth), "ctx", split_axis=0, concat_axis=0, tiled=True
     )

time: 384 us -> 314 us (0.82)
  waiting for transfers between devices: 206 us -> 151 us
  blocking collectives: 87.3 us -> 56.9 us
  starting transfers between devices: 10.7 us -> 19.2 us
  matrix products: 45.1 us -> 50.7 us
    reduce_scatter x3 -> x0, waiting for transfers between devices: 97.5 us -> none  [the longest x1 46.4 us: body(): lax.psum_scatter(up_part.astype(jnp.bfloat16), 'tp', scatter_dimension=1,...]
    ppermute x0 -> x14, waiting for transfers between devices: none -> 67.6 us  [the longest x12 63.2 us: swapped(): lax.ppermute(value, 'tp', [(p, p ^ distance) for p in range(lax.axis_size...]
    all_gather x2 -> x1, waiting for transfers between devices: 90.7 us -> 47.5 us  [body(): lax.all_gather((gated * mixer_gain[None, :]).astype(jnp.bfloat16), 'ctx',...]
    all_to_all x1 -> x0, blocking collectives: 23 us -> none  [body(): lax.all_to_all(outgoing, 'ctx', split_axis=0, concat_axis=0, tiled=True)]
    all_gather x2 -> x1, blocking collectives: 52.6 us -> 33.3 us  [entering(): everything = lax.all_gather(packed, axis).astype(jnp.float32)]
    all_to_all x0 -> x1, waiting for transfers between devices: none -> 17.6 us  [body(): lax.all_to_all(outgoing, 'ctx', split_axis=0, concat_axis=0, tiled=True)]
    psum x1, blocking collectives: 5.75 us -> 16.4 us  [body(): feed_sum = lax.psum(jnp.sum(state_float * state_float, axis=1), 'tp')]
    ppermute x0 -> x14, starting transfers between devices: none -> 6.74 us  [the longest x12 5.45 us: swapped(): lax.ppermute(value, 'tp', [(p, p ^ distance) for p in range(lax.axis_size...]
  transfers between devices with their start and end apart: 7 -> 18, of which waited for: 6 -> 9; matrix products, arithmetic and copies ran while one was open for 7% -> 14% of each run, Pallas kernels for 0% -> 0%
where the time goes in v1:
time: 314 us
  waiting for transfers between devices  151 us (48%)
  blocking collectives  56.9 us (18%)
  matrix products  50.7 us (16%)
  starting transfers between devices  19.2 us (6%)
  between operations  14.1 us (4%)
  other arithmetic  11.8 us (4%)
  local copies, waits for them, and re-layouts  9.91 us (3%)
    ppermute x12, waiting for transfers between devices, swapped(): lax.ppermute(value, 'tp', [(p, p ^ distance) for p in range(lax.axis_size...  63.2 us
    all_gather x1, waiting for transfers between devices, body(): lax.all_gather((gated * mixer_gain[None, :]).astype(jnp.bfloat16), 'ctx',...  47.5 us
    dot_general x8, matrix products, product(): return jnp.dot(flattened, columns, preferred_element_type=jnp.float32)  33.5 us
    all_gather x1, blocking collectives, entering(): everything = lax.all_gather(packed, axis).astype(jnp.float32)  33.3 us
    all_to_all x1, waiting for transfers between devices, body(): lax.all_to_all(outgoing, 'ctx', split_axis=0, concat_axis=0, tiled=True)  17.6 us
    all_to_all x1, waiting for transfers between devices, body(): lax.all_to_all(answer.reshape(sources, items, depth), 'ctx', split_axis=0...  16.4 us
    psum x1, blocking collectives, body(): feed_sum = lax.psum(jnp.sum(state_float * state_float, axis=1), 'tp')  16.4 us
    dot_general x4, matrix products, lowered(): return jnp.dot(part, rows, preferred_element_type=jnp.float32)  7.29 us
  transfers between devices with their start and end apart: 18, of which 9 were waited for; matrix products, arithmetic and copies ran while one was open for 14% of the time, Pallas kernels for 0%

profile of v1, /device:TPU:0, one launch (start us, length us, event | category | flops | bytes accessed | tf_op | source)
XLA Modules:
  0.0 313.6 jit_solution(7496549109479400627)
XLA Ops:
  6.5 1.2 copy.74
  7.8 0.8 fusion.115
  8.6 4.9 %collective-permute-start = (bf16[3,1056]{0,1:T(8,128)(2,1)S(1)}, bf16[3,1056]{0,1:T(8,128)(2,1)S(1)}, u32[]{:S(2)}, u32[]{:S(2)}) collective-permute-start(bf16[3,1056]{0,1:T(8,128)(2,1)S(1)} %fusion.115), channel_id=1, source_target_pairs={{0,4},{4,8},{8,12},{12,16},{16,20},{20,24},{24,28},{1,5},{5,9},{9,... | collective-permute-start | bytes 19016 | tf_op jit(solution)/shard_map/ppermute | solution.py:16
  13.5 0.7 fusion.114
  14.9 0.8 negate_multiply_fusion
  17.7 1.5 collective-permute-done
  19.2 1.5 divide_multiply_fusion
  21.6 33.3 %all_gather.7 = bf16[8,17,1024]{2,1,0:T(8,128)(2,1)S(1)} all-gather(bf16[1,17,1024]{2,1,0:T(8,128)(2,1)S(1)} %pad_maximum_fusion.2), channel_id=1, replica_groups=mesh['ctx'=8,'tp'=4] {'ctx'}, dimensions={0}, use_global_device_ids=true | all-gather | bytes 313344 | tf_op jit(solution)/shard_map/all_gather | solution.py:26
  55.6 1.0 fusion.125
  56.6 3.0 fusion.75
  59.9 0.9 multiply_reduce_fusion.1
  62.5 47.5 %all-gather.2.cloned.1.call-done = bf16[1024,1024]{1,0:T(8,128)(2,1)} async-done(((bf16[128,1024]{1,0:T(8,128)(2,1)}), bf16[1024,1024]{1,0:T(8,128)(2,1)}) %all-gather.2.cloned.1.call-update) | async-done | bytes 2097168 | tf_op jit(solution)/shard_map/all_gather | solution.py:109
  110.0 2.3 convolution_convert_fusion.1
  112.4 7.2 %psum.14 = f32[128]{0:T(128)S(1)} all-reduce(f32[128]{0:T(128)S(1)} %get-tuple-element.116), channel_id=1, replica_groups=mesh['ctx'=8,'tp'=4] {'tp'}, use_global_device_ids=true, to_apply=%region_4.5 | all-reduce | flops 128 | bytes 1024 | tf_op jit(solution)/shard_map/psum | solution.py:112
  119.7 1.5 convolution_convert_fusion.2
  122.8 7.7 %collective-permute-done.3 = bf16[256,512]{1,0:T(8,128)(2,1)S(1)} collective-permute-done((bf16[256,512]{1,0:T(8,128)(2,1)S(1)}, bf16[256,512]{1,0:T(8,128)(2,1)S(1)}, u32[]{:S(2)}, u32[]{:S(2)}) %collective-permute-start.3) | collective-permute-done | bytes 262176 | tf_op jit(solution)/shard_map/ppermute | solution.py:20
  130.6 0.7 collective-permute-start.4
  131.9 4.4 %collective-permute-done.5 = bf16[128,512]{1,0:T(8,128)(2,1)S(1)} collective-permute-done((bf16[128,512]{1,0:T(8,128)(2,1)S(1)}, bf16[128,512]{1,0:T(8,128)(2,1)S(1)}, u32[]{:S(2)}, u32[]{:S(2)}) %collective-permute-start.5) | collective-permute-done | bytes 131104 | tf_op jit(solution)/shard_map/ppermute | solution.py:137
  136.6 16.4 %psum.15 = f32[128]{0:T(128)S(1)} all-reduce(f32[128]{0:T(128)S(1)} %fusion.95), channel_id=1, replica_groups=mesh['ctx'=8,'tp'=4] {'tp'}, use_global_device_ids=true, to_apply=%region_10.11 | all-reduce | flops 128 | bytes 1024 | tf_op jit(solution)/shard_map/psum | solution.py:151
  153.4 1.0 reshape_reshape.3
  154.4 4.0 %all-to-all-start = ((bf16[8,36,1024]{2,1,0:T(8,128)(2,1)}), bf16[8,36,1024]{2,1,0:T(8,128)(2,1)S(1)}, u32[]{:S(2)}, u32[]{:S(2)}) async-start(bf16[8,36,1024]{2,1,0:T(8,128)(2,1)} %reshape_reshape.3), calls=%async_computation | async-start | bytes 1310720 | tf_op jit(solution)/shard_map/all_to_all | solution.py:171
  158.4 17.6 %all-to-all-done = bf16[8,36,1024]{2,1,0:T(8,128)(2,1)S(1)} async-done(((bf16[8,36,1024]{2,1,0:T(8,128)(2,1)}), bf16[8,36,1024]{2,1,0:T(8,128)(2,1)S(1)}, u32[]{:S(2)}, u32[]{:S(2)}) %all-to-all-start) | async-done | bytes 589856 | tf_op jit(solution)/shard_map/all_to_all | solution.py:171
  176.1 4.5 %fusion.47 = bf16[288,1792]{1,0:T(8,128)(2,1)} fusion(bf16[288,1024]{1,0:T(8,128)(2,1)S(1)} %reshape.144, bf16[1,1024,7168]{2,1,0:T(8,128)(2,1)} %param.33, s32[]{:T(128)S(6)} %select_n.133), kind=kOutput, calls=%fused_computation.44 | convolution fusion | flops 1057480704 | bytes 5292036 | tf_op jit(solution)/shard_map/dot_general | solution.py:178
  180.5 4.2 %fusion.59 = bf16[288,1792]{1,0:T(8,128)(2,1)} fusion(bf16[288,1024]{1,0:T(8,128)(2,1)S(1)} %reshape.144, bf16[1,1024,7168]{2,1,0:T(8,128)(2,1)} %param.34, s32[]{:T(128)S(6)} %select_n.133), kind=kOutput, calls=%fused_computation.48 | convolution fusion | flops 1057480704 | bytes 5292036 | tf_op jit(solution)/shard_map/dot_general | solution.py:178
  185.3 4.3 %fusion.44 = bf16[288,1792]{1,0:T(8,128)(2,1)} fusion(bf16[288,1024]{1,0:T(8,128)(2,1)S(1)} %reshape.144, bf16[1,1024,7168]{2,1,0:T(8,128)(2,1)} %param.33, s32[]{:T(128)S(6)} %select_n.131), kind=kOutput, calls=%fused_computation.43 | convolution fusion | flops 1057480704 | bytes 5292036 | tf_op jit(solution)/shard_map/dot_general | solution.py:178
  189.6 4.2 %fusion.56 = bf16[288,1792]{1,0:T(8,128)(2,1)} fusion(bf16[288,1024]{1,0:T(8,128)(2,1)S(1)} %reshape.144, bf16[1,1024,7168]{2,1,0:T(8,128)(2,1)} %param.34, s32[]{:T(128)S(6)} %select_n.131), kind=kOutput, calls=%fused_computation.47 | convolution fusion | flops 1057480704 | bytes 5292036 | tf_op jit(solution)/shard_map/dot_general | solution.py:178
  194.3 4.5 %add_convert_fusion.1 = bf16[288,1792]{1,0:T(8,128)(2,1)} fusion(bf16[288,1792]{1,0:T(8,128)(2,1)} %collective-permute-done.7, bf16[288,1024]{1,0:T(8,128)(2,1)S(1)} %reshape.144, bf16[1,1024,7168]{2,1,0:T(8,128)(2,1)} %param.33, s32[]{:T(128)S(6)} %select_n.132), kind=kOutput, calls=%fused_computation.51 | convolution fusion | flops 1058512896 | bytes 6324228 | tf_op jit(solution)/shard_map/dot_general | solution.py:178
  198.9 1.6 collective-permute-start.8
  200.5 4.7 %add_convert_fusion = bf16[288,1792]{1,0:T(8,128)(2,1)} fusion(bf16[288,1792]{1,0:T(8,128)(2,1)} %collective-permute-done.10, bf16[288,1024]{1,0:T(8,128)(2,1)} %copy-done.3, bf16[1,1024,7168]{2,1,0:T(8,128)(2,1)} %param.34, s32[]{:T(128)S(6)} %select_n.132), kind=kOutput, calls=%fused_computation.50 | convolution fusion | flops 1058512896 | bytes 6324228 | tf_op jit(solution)/shard_map/dot_general | solution.py:178
  205.6 3.6 %fusion.41 = f32[288,1792]{1,0:T(8,128)S(1)} fusion(bf16[288,1024]{1,0:T(8,128)(2,1)} %copy-done.3, bf16[1,1024,7168]{2,1,0:T(8,128)(2,1)} %param.33, s32[]{:T(128)S(6)} %select_n.130), kind=kOutput, calls=%fused_computation.42 | convolution fusion | flops 1057996800 | bytes 6324228 | tf_op jit(solution)/shard_map/dot_general | solution.py:178
  209.3 3.4 %fusion.53 = f32[288,1792]{1,0:T(8,128)S(1)} fusion(bf16[288,1024]{1,0:T(8,128)(2,1)S(1)} %copy-done.4, bf16[1,1024,7168]{2,1,0:T(8,128)(2,1)} %param.34, s32[]{:T(128)S(6)} %select_n.130), kind=kOutput, calls=%fused_computation.46 | convolution fusion | flops 1057996800 | bytes 6324228 | tf_op jit(solution)/shard_map/dot_general | solution.py:178
  212.7 12.0 %collective-permute-done.8 = bf16[288,1792]{1,0:T(8,128)(2,1)S(1)} collective-permute-done((bf16[288,1792]{1,0:T(8,128)(2,1)}, bf16[288,1792]{1,0:T(8,128)(2,1)S(1)}, u32[]{:S(2)}, u32[]{:S(2)}) %collective-permute-start.8) | collective-permute-done | bytes 1032224 | tf_op jit(solution)/shard_map/ppermute | solution.py:20
  224.8 21.3 %collective-permute-done.11 = bf16[288,1792]{1,0:T(8,128)(2,1)} collective-permute-done((bf16[288,1792]{1,0:T(8,128)(2,1)}, bf16[288,1792]{1,0:T(8,128)(2,1)}, u32[]{:S(2)}, u32[]{:S(2)}) %collective-permute-start.11) | collective-permute-done | bytes 1032224 | tf_op jit(solution)/shard_map/ppermute | solution.py:20
  246.0 2.3 multiply_convert_fusion
  248.3 1.7 collective-permute-start.13
  250.0 22.2 %collective-permute-done.13 = bf16[288,1792]{1,0:T(8,128)(2,1)S(1)} collective-permute-done((bf16[288,1792]{1,0:T(8,128)(2,1)S(1)}, bf16[288,1792]{1,0:T(8,128)(2,1)S(1)}, u32[]{:S(2)}, u32[]{:S(2)}) %collective-permute-start.13) | collective-permute-done | bytes 1032224 | tf_op jit(solution)/shard_map/ppermute | solution.py:20
  272.3 3.3 %fusion.4 = f32[288,1024]{1,0:T(8,128)S(1)} fusion(bf16[288,1792]{1,0:T(8,128)(2,1)S(1)} %collective-permute-done.13, bf16[1,7168,1024]{2,1,0:T(8,128)(2,1)} %param.35, s32[]{:T(128)S(6)} %select_n.132), kind=kOutput, calls=%fused_computation.7 | convolution fusion | flops 1056964608 | bytes 5881860 | tf_op jit(solution)/shard_map/dot_general | solution.py:200
  275.6 1.3 fusion.6
  276.9 1.5 fusion.68
  278.4 1.3 fusion.71
  279.6 1.0 reshape.145
  280.6 3.6 %all-to-all-start.1 = ((bf16[8,36,1024]{2,1,0:T(8,128)(2,1)}), bf16[8,36,1024]{2,1,0:T(8,128)(2,1)S(1)}, u32[]{:S(2)}, u32[]{:S(2)}) async-start(bf16[8,36,1024]{2,1,0:T(8,128)(2,1)} %reshape.145), calls=%async_computation.1 | async-start | bytes 1310720 | tf_op jit(solution)/shard_map/all_to_all | solution.py:208
  284.5 0.7 copy.86
  285.2 0.7 copy.82
  286.0 16.4 %all-to-all-done.1 = bf16[8,36,1024]{2,1,0:T(8,128)(2,1)S(1)} async-done(((bf16[8,36,1024]{2,1,0:T(8,128)(2,1)}), bf16[8,36,1024]{2,1,0:T(8,128)(2,1)S(1)}, u32[]{:S(2)}, u32[]{:S(2)}) %all-to-all-start.1) | async-done | bytes 589856 | tf_op jit(solution)/shard_map/all_to_all | solution.py:208
  302.5 1.1 gather_fusion
  304.4 1.5 multiply_reduce_fusion
  306.0 0.8 fusion.98
  (135 shorter events, 12.1 us)
Async XLA Ops:
  6.5 103.5 %copy-start = (bf16[1024,512]{1,0:T(8,128)(2,1)S(1)}, bf16[1024,512]{1,0:T(8,128)(2,1)}, u32[]{:S(2)}) copy-start(bf16[1024,512]{1,0:T(8,128)(2,1)} %param.31) | copy-start | bytes 3145732
  6.5 9.5 %copy-start.11 = (f32[4,1024]{1,0:T(4,128)S(1)}, f32[4,1024]{1,0:T(4,128)}, u32[]{:S(2)}) copy-start(f32[4,1024]{1,0:T(4,128)} %param.25) | copy-start | bytes 49156
  6.5 9.5 %copy-start.15 = (f32[4,32]{1,0:T(4,128)S(1)}, f32[4,32]{1,0:T(4,128)}, u32[]{:S(2)}) copy-start(f32[4,32]{1,0:T(4,128)} %param.26) | copy-start | bytes 1540
  6.5 103.5 %all-gather.2.cloned.1.call-start = ((), (), s32[]{:S(2)}) async-start(), calls=%async_computation.2 | async-start | bytes 2359296 | tf_op jit(solution)/shard_map/all_gather | solution.py:109
  8.6 10.6 %collective-permute-start = (bf16[3,1056]{0,1:T(8,128)(2,1)S(1)}, bf16[3,1056]{0,1:T(8,128)(2,1)S(1)}, u32[]{:S(2)}, u32[]{:S(2)}) collective-permute-start(bf16[3,1056]{0,1:T(8,128)(2,1)S(1)} %fusion.115), channel_id=1, source_target_pairs={{0,4},{4,8},{8,12},{12,16},{16,20},{20,24},{24,28},{1,5},{5,9},{9,... | collective-permute-start | bytes 19016 | tf_op jit(solution)/shard_map/ppermute | solution.py:16
  15.7 1.2 copy-start.9
  16.0 0.8 copy-start.10
  55.6 4.3 %copy-start.6 = (bf16[128,1024]{1,0:T(8,128)(2,1)S(1)}, bf16[128,1024]{1,0:T(8,128)(2,1)}, u32[]{:S(2)}) copy-start(bf16[128,1024]{1,0:T(8,128)(2,1)} %param.22) | copy-start | bytes 786436
  56.6 3.3 %copy-start.12 = (f32[1024]{0:T(1024)S(1)}, f32[1024]{0:T(1024)}, u32[]{:S(2)}) copy-start(f32[1024]{0:T(1024)} %param.30) | copy-start | bytes 12292
  56.6 4.2 %copy-start.14 = (s32[128,2]{0,1:T(2,128)S(1)}, s32[128,2]{0,1:T(2,128)}, u32[]{:S(2)}) copy-start(s32[128,2]{0,1:T(2,128)} %param.36) | copy-start | bytes 3076
  110.0 11.2 %copy-start.2 = (bf16[1024,1024]{1,0:T(8,128)(2,1)S(1)}, bf16[1024,1024]{1,0:T(8,128)(2,1)}, u32[]{:S(2)}) copy-start(bf16[1024,1024]{1,0:T(8,128)(2,1)} %all-gather.2.cloned.1.call-done) | copy-start | bytes 6291460
  112.3 8.9 %collective-permute-start.2 = (bf16[256,512]{1,0:T(8,128)(2,1)}, bf16[256,512]{1,0:T(8,128)(2,1)S(1)}, u32[]{:S(2)}, u32[]{:S(2)}) collective-permute-start(bf16[256,512]{1,0:T(8,128)(2,1)} %convolution_convert_fusion.1), channel_id=1, source_target_pairs={{0,1},{1,0},{2,3},{3,2},{4,5},{5,4},{6,7},{7,6},{8,9},{9,8},{10,11... | collective-permute-start | bytes 786440 | tf_op jit(solution)/shard_map/ppermute | solution.py:20
  121.2 1.6 collective-permute-start.1
  121.7 14.7 %copy-start.7 = (bf16[128,1024]{1,0:T(8,128)(2,1)S(1)}, bf16[128,1024]{1,0:T(8,128)(2,1)}, u32[]{:S(2)}) copy-start(bf16[128,1024]{1,0:T(8,128)(2,1)} %param.20) | copy-start | bytes 786436
  121.7 8.8 %collective-permute-start.3 = (bf16[256,512]{1,0:T(8,128)(2,1)S(1)}, bf16[256,512]{1,0:T(8,128)(2,1)S(1)}, u32[]{:S(2)}, u32[]{:S(2)}) collective-permute-start(bf16[256,512]{1,0:T(8,128)(2,1)S(1)} %add_convert_fusion.4), channel_id=1, source_target_pairs={{0,2},{1,3},{2,0},{3,1},{4,6},{5,7},{6,4},{7,5},{8,10},{9,11},{10,... | collective-permute-start | bytes 786440 | tf_op jit(solution)/shard_map/ppermute | solution.py:20
  122.8 30.3 %copy-start.13 = (f32[1024]{0:T(1024)S(1)}, f32[1024]{0:T(1024)}, u32[]{:S(2)}) copy-start(f32[1024]{0:T(1024)} %param.32) | copy-start | bytes 12292
  130.6 1.3 collective-permute-start.4
  131.3 5.0 %collective-permute-start.5 = (bf16[128,512]{1,0:T(8,128)(2,1)S(1)}, bf16[128,512]{1,0:T(8,128)(2,1)S(1)}, u32[]{:S(2)}, u32[]{:S(2)}) collective-permute-start(bf16[128,512]{1,0:T(8,128)(2,1)S(1)} %get-tuple-element.123), channel_id=1, source_target_pairs={{0,4},{1,12},{2,20},{3,28},{4,0},{5,8},{6,16},{7,24},{8,5},{9,13},... | collective-permute-start | bytes 393224 | tf_op jit(solution)/shard_map/ppermute | solution.py:137
  154.4 21.6 %all-to-all-start = ((bf16[8,36,1024]{2,1,0:T(8,128)(2,1)}), bf16[8,36,1024]{2,1,0:T(8,128)(2,1)S(1)}, u32[]{:S(2)}, u32[]{:S(2)}) async-start(bf16[8,36,1024]{2,1,0:T(8,128)(2,1)} %reshape_reshape.3), calls=%async_computation | async-start | bytes 1310720 | tf_op jit(solution)/shard_map/all_to_all | solution.py:171
  176.1 18.3 %copy-start.3 = (bf16[288,1024]{1,0:T(8,128)(2,1)}, bf16[288,1024]{1,0:T(8,128)(2,1)S(1)}, u32[]{:S(2)}) copy-start(bf16[288,1024]{1,0:T(8,128)(2,1)S(1)} %reshape.144) | copy-start | bytes 1769476
  180.5 13.8 %collective-permute-start.7 = (bf16[288,1792]{1,0:T(8,128)(2,1)}, bf16[288,1792]{1,0:T(8,128)(2,1)}, u32[]{:S(2)}, u32[]{:S(2)}) collective-permute-start(bf16[288,1792]{1,0:T(8,128)(2,1)} %fusion.47), channel_id=1, source_target_pairs={{0,1},{1,0},{2,3},{3,2},{4,5},{5,4},{6,7},{7,6},{8,9},{9,8},{10,11... | collective-permute-start | bytes 3096584 | tf_op jit(solution)/shard_map/ppermute | solution.py:20
  184.8 15.7 %collective-permute-start.10 = (bf16[288,1792]{1,0:T(8,128)(2,1)}, bf16[288,1792]{1,0:T(8,128)(2,1)}, u32[]{:S(2)}, u32[]{:S(2)}) collective-permute-start(bf16[288,1792]{1,0:T(8,128)(2,1)} %fusion.59), channel_id=1, source_target_pairs={{0,1},{1,0},{2,3},{3,2},{4,5},{5,4},{6,7},{7,6},{8,9},{9,8},{10,11... | collective-permute-start | bytes 3096584 | tf_op jit(solution)/shard_map/ppermute | solution.py:20
  189.6 23.1 %collective-permute-start.6 = (bf16[288,1792]{1,0:T(8,128)(2,1)}, bf16[288,1792]{1,0:T(8,128)(2,1)S(1)}, u32[]{:S(2)}, u32[]{:S(2)}) collective-permute-start(bf16[288,1792]{1,0:T(8,128)(2,1)} %fusion.44), channel_id=1, source_target_pairs={{0,1},{1,0},{2,3},{3,2},{4,5},{5,4},{6,7},{7,6},{8,9},{9,8},{10,11... | collective-permute-start | bytes 3096584 | tf_op jit(solution)/shard_map/ppermute | solution.py:20
  193.8 18.9 %collective-permute-start.9 = (bf16[288,1792]{1,0:T(8,128)(2,1)}, bf16[288,1792]{1,0:T(8,128)(2,1)S(1)}, u32[]{:S(2)}, u32[]{:S(2)}) collective-permute-start(bf16[288,1792]{1,0:T(8,128)(2,1)} %fusion.56), channel_id=1, source_target_pairs={{0,1},{1,0},{2,3},{3,2},{4,5},{5,4},{6,7},{7,6},{8,9},{9,8},{10,11... | collective-permute-start | bytes 3096584 | tf_op jit(solution)/shard_map/ppermute | solution.py:20
  198.9 25.9 %collective-permute-start.8 = (bf16[288,1792]{1,0:T(8,128)(2,1)}, bf16[288,1792]{1,0:T(8,128)(2,1)S(1)}, u32[]{:S(2)}, u32[]{:S(2)}) collective-permute-start(bf16[288,1792]{1,0:T(8,128)(2,1)} %add_convert_fusion.1), channel_id=1, source_target_pairs={{0,2},{1,3},{2,0},{3,1},{4,6},{5,7},{6,4},{7,5},{8,10},{9,11},{10,... | collective-permute-start | bytes 3096584 | tf_op jit(solution)/shard_map/ppermute | solution.py:20
  205.2 40.8 %collective-permute-start.11 = (bf16[288,1792]{1,0:T(8,128)(2,1)}, bf16[288,1792]{1,0:T(8,128)(2,1)}, u32[]{:S(2)}, u32[]{:S(2)}) collective-permute-start(bf16[288,1792]{1,0:T(8,128)(2,1)} %add_convert_fusion), channel_id=1, source_target_pairs={{0,2},{1,3},{2,0},{3,1},{4,6},{5,7},{6,4},{7,5},{8,10},{9,11},{10,... | collective-permute-start | bytes 3096584 | tf_op jit(solution)/shard_map/ppermute | solution.py:20
  205.6 3.6 %copy-start.4 = (bf16[288,1024]{1,0:T(8,128)(2,1)S(1)}, bf16[288,1024]{1,0:T(8,128)(2,1)}, u32[]{:S(2)}) copy-start(bf16[288,1024]{1,0:T(8,128)(2,1)} %copy-done.3) | copy-start | bytes 1769476
  205.6 69.9 %slice-start = ((s8[14680064]{0:T(1024)(128)(4,1)}), s8[4194304]{0:T(1024)(128)(4,1)S(1)}, s32[]{:S(2)}) async-start(s8[14680064]{0:T(1024)(128)(4,1)} %bitcast.130), calls=%async_computation.3 | async-start | bytes 8388608
  209.2 66.3 %slice-start.1 = ((s8[14680064]{0:T(1024)(128)(4,1)}), s8[4194304]{0:T(1024)(128)(4,1)S(1)}, s32[]{:S(2)}) async-start(s8[14680064]{0:T(1024)(128)(4,1)} %bitcast.130), calls=%async_computation.4 | async-start | bytes 8388608
  212.7 62.9 %slice-start.2 = ((s8[14680064]{0:T(1024)(128)(4,1)}), s8[4194304]{0:T(1024)(128)(4,1)S(1)}, s32[]{:S(2)}) async-start(s8[14680064]{0:T(1024)(128)(4,1)} %bitcast.130), calls=%async_computation.5 | async-start | bytes 8388608
  212.7 62.9 %slice-start.3 = ((s8[14680064]{0:T(1024)(128)(4,1)}), s8[2097152]{0:T(1024)(128)(4,1)S(1)}, s32[]{:S(2)}) async-start(s8[14680064]{0:T(1024)(128)(4,1)} %bitcast.130), calls=%async_computation.6 | async-start | bytes 4194304
  248.3 23.9 %collective-permute-start.13 = (bf16[288,1792]{1,0:T(8,128)(2,1)S(1)}, bf16[288,1792]{1,0:T(8,128)(2,1)S(1)}, u32[]{:S(2)}, u32[]{:S(2)}) collective-permute-start(bf16[288,1792]{1,0:T(8,128)(2,1)S(1)} %multiply_convert_fusion), channel_id=1, source_target_pairs={{0,2},{1,3},{2,0},{3,1},{4,6},{5,7},{6,4},{7,5},{8,10},{9,11},{10,... | collective-permute-start | bytes 3096584 | tf_op jit(solution)/shard_map/ppermute | solution.py:20
  250.0 25.5 %collective-permute-start.12 = (bf16[288,1792]{1,0:T(8,128)(2,1)S(1)}, bf16[288,1792]{1,0:T(8,128)(2,1)S(1)}, u32[]{:S(2)}, u32[]{:S(2)}) collective-permute-start(bf16[288,1792]{1,0:T(8,128)(2,1)S(1)} %multiply_convert_fusion), channel_id=1, source_target_pairs={{0,1},{1,0},{2,3},{3,2},{4,5},{5,4},{6,7},{7,6},{8,9},{9,8},{10,11... | collective-permute-start | bytes 3096584 | tf_op jit(solution)/shard_map/ppermute | solution.py:20
  272.2 6.1 %collective-permute-start.14 = (bf16[288,1792]{1,0:T(8,128)(2,1)S(1)}, bf16[288,1792]{1,0:T(8,128)(2,1)S(1)}, u32[]{:S(2)}, u32[]{:S(2)}) collective-permute-start(bf16[288,1792]{1,0:T(8,128)(2,1)S(1)} %collective-permute-done.13), channel_id=1, source_target_pairs={{0,1},{1,0},{2,3},{3,2},{4,5},{5,4},{6,7},{7,6},{8,9},{9,8},{10,11... | collective-permute-start | bytes 3096584 | tf_op jit(solution)/shard_map/ppermute | solution.py:20
  279.6 5.6 %copy-start.16 = (f32[128,2]{0,1:T(2,128)S(1)}, f32[128,2]{0,1:T(2,128)}, u32[]{:S(2)}) copy-start(f32[128,2]{0,1:T(2,128)} %param.37) | copy-start | bytes 3076
  280.6 21.8 %all-to-all-start.1 = ((bf16[8,36,1024]{2,1,0:T(8,128)(2,1)}), bf16[8,36,1024]{2,1,0:T(8,128)(2,1)S(1)}, u32[]{:S(2)}, u32[]{:S(2)}) async-start(bf16[8,36,1024]{2,1,0:T(8,128)(2,1)} %reshape.145), calls=%async_computation.1 | async-start | bytes 1310720 | tf_op jit(solution)/shard_map/all_to_all | solution.py:208
  302.5 4.3 %copy-start.1 = (bf16[1024,512]{1,0:T(8,128)(2,1)S(1)}, bf16[1024,512]{1,0:T(8,128)(2,1)}, u32[]{:S(2)}) copy-start(bf16[1024,512]{1,0:T(8,128)(2,1)} %param.31) | copy-start | bytes 3145732
  303.6 0.8 copy-start.5
  303.6 0.8 copy-start.8
Sparse Core Ops, SparseCore 0:
  60.9 49.0 all-gather.1
